TPU v7x, 128 devices: a whole 4x4x4 slice. The times are simulated.
128 devices in a mesh: tile: 16 (over x_lo, z, core), chan: 8 (over y, x_hi).
Axes of the slice: x: 4 (x_hi: 2, x_lo: 2; x = x_hi * 2 + x_lo), y: 4, z: 4, core: 2. Of those that a mesh axis runs over, the one named last changes fastest.
Arguments:
- voltages: int32 [512, 262144], P('tile', 'chan'), may hold values from -128 to 127
- history: int32 [512, 30720], P('tile'), may hold values from -128 to 127
- filter_taps: int32 [16, 2048], replicated, may hold values from -64 to 64
Outputs:
- visibilities: float32 [2, 1024, 512, 512], P(None, 'chan', 'tile')
Inputs may be any that keep to these rules, and one draw needn't show every extreme that they name: `voltages`: 8-bit signed samples. `history`: 8-bit signed samples.
All inputs are finite; a program needn't handle non-finite values.
Results may differ from a plain program's by a relative error of at most 0.006.
Values may be sent and summed in bfloat16 or wider, within the bound.
A program may use at most 192 MiB of HBM per device.

v0:
```python
import math
import jax
import jax.numpy as jnp
from jax import lax
from jax.sharding import PartitionSpec as P

CH = 1024
TAPS = 16
FFT = 2048
filter_norm = 1.0 / 16384.0


def from_behind(value, axis, steps):
    count = lax.axis_size(axis)
    leading, last = (max(0, -steps), min(count, count - steps))
    return lax.ppermute(value, axis, [(source, source + steps) for source in range(leading, last)])


def dft_table(samples, channels):
    rows_index = jnp.arange(samples, dtype=jnp.int32)[:, None]
    cols_index = jnp.arange(channels, dtype=jnp.int32)[None, :]
    angles = (rows_index * cols_index % samples).astype(jnp.float32) * (2.0 * math.pi / samples)
    factor = 1.0 / math.sqrt(channels)
    return jnp.concatenate([jnp.cos(angles) * factor, -jnp.sin(angles) * factor], axis=1).astype(
        jnp.bfloat16
    )


def polyphase(extended, weights, spectra_count):
    summed = jnp.zeros((extended.shape[0], spectra_count, extended.shape[2]), jnp.float32)
    for tap_index in range(weights.shape[0]):
        summed = (
            summed
            + weights[tap_index][None, None, :]
            * extended[:, tap_index : tap_index + spectra_count, :]
        )
    return summed


def counter_rows(spectra):
    real_part = spectra[:, :, 0]
    imag_part = spectra[:, :, 1]
    rotated = jnp.stack([imag_part, -real_part], axis=2)
    return jnp.stack([spectra, rotated], axis=0)


def body(voltages, history, filter_taps):
    local_inputs = voltages.shape[0]
    spectra_count = voltages.shape[1] // FFT
    tail_blocks = voltages[:, (spectra_count - TAPS + 1) * FFT :].astype(jnp.bfloat16)
    carried = from_behind(tail_blocks, "chan", 1)
    is_first = lax.axis_index("chan") == 0
    earlier = jnp.where(is_first, history.astype(jnp.float32), carried.astype(jnp.float32))
    extended = jnp.concatenate([earlier, voltages.astype(jnp.float32)], axis=1)
    extended = extended.reshape(local_inputs, spectra_count + TAPS - 1, FFT)
    filtered = (
        polyphase(extended, filter_taps.astype(jnp.float32), spectra_count) * filter_norm
    ).astype(jnp.bfloat16)
    spectra = jnp.dot(
        filtered.reshape(-1, FFT), dft_table(FFT, CH), preferred_element_type=jnp.float32
    )
    spectra = spectra.reshape(local_inputs, spectra_count, 2, CH).astype(jnp.bfloat16)
    turned = lax.all_to_all(spectra, "chan", split_axis=3, concat_axis=1, tiled=True)
    total_spectra = turned.shape[1]
    average = 1.0 / total_spectra
    row_sets = counter_rows(turned)
    return (
        jnp.einsum(
            "qaspc,bspc->qcab",
            row_sets,
            lax.all_gather(turned, "tile", axis=0, tiled=True),
            preferred_element_type=jnp.float32,
        )
        * average
    )


def solution(mesh):
    in_specs = (P("tile", "chan"), P("tile", None), P())
    out_specs = P(None, "chan", "tile", None)
    return jax.shard_map(body, mesh=mesh, in_specs=in_specs, out_specs=out_specs, check_vma=False)
```

profile of v0, /device:TPU:1, one launch (start us, length us, event | category | flops | bytes accessed | tf_op | source)
XLA Modules:
  0.0 409.3 jit_solution(11984337973401259222)
XLA Ops:
  6.5 0.0 copy-start.3
  6.5 0.0 all-gather.2.cloned.1.call-start
  6.5 0.0 copy-start.1
  6.5 3.7 slice_convert_fusion
  10.3 5.6 %collective-permute-start = (bf16[32,30720]{1,0:T(8,128)(2,1)}, bf16[32,30720]{1,0:T(8,128)(2,1)S(1)}, u32[]{:S(2)}, u32[]{:S(2)}) collective-permute-start(bf16[32,30720]{1,0:T(8,128)(2,1)} %slice_convert_fusion), channel_id=1, source_target_pairs={{0,1},{1,2},{2,3},{3,4},{4,5},{5,6},{6,7},{8,9},{9,10},{10,11},{11... | collective-permute-start | bytes 5898248 | tf_op jit(solution)/shard_map/ppermute | solution.py:16
  15.9 0.0 copy-done.3
  15.9 0.1 fusion.40
  16.0 0.0 copy-done.1
  16.0 2.2 convert_element_type.28
  18.2 34.9 %multiply_convert_fusion = (bf16[2048,1024]{0,1:T(8,128)(2,1)}, bf16[2048,1024]{0,1:T(8,128)(2,1)}) fusion(), kind=kLoop, calls=%fused_computation.11 | loop fusion | flops 39845888 | bytes 8388608 | tf_op jit(solution)/shard_map/convert.1
  53.2 8.5 %pad_maximum_fusion = bf16[2048,2048]{0,1:T(8,128)(2,1)} fusion(bf16[2048,1024]{0,1:T(8,128)(2,1)} %get-tuple-element.23, bf16[2048,1024]{0,1:T(8,128)(2,1)} %get-tuple-element.24), kind=kLoop, calls=%fused_computation.10 | loop fusion | flops 16777216 | bytes 16777216 | tf_op jit(solution)/shard_map/concatenate | solution.py:24
  61.7 0.0 copy-start
  61.7 0.0 collective-permute-done
  61.7 2.6 convert_select_fusion
  64.4 0.7 copy-done
  65.1 3.7 pad_maximum_fusion.1
  68.7 7.6 %reshape.25 = f32[32,31,2048]{2,1,0:T(8,128)} reshape(f32[32,63488]{1,0:T(8,128)} %pad_maximum_fusion.1) | data formatting | bytes 16252928 | tf_op jit(solution)/shard_map/reshape | solution.py:55
  76.4 43.5 %fusion.34 = bf16[32,16,2,1024]{3,1,2,0:T(8,128)(2,1)S(1)} fusion(bf16[2,1024,2048,1]{2,1,0,3:T(8,128)(2,1)} %bitcast.59, f32[32,31,2048]{2,1,0:T(8,128)} %reshape.25, f32[2048]{0:T(1024)S(1)} %bitcast.61, f32[2048]{0:T(1024)S(1)} %bitcast.62, f32[2048]{0:T(1024)S(1)} %bitcast.63, f32[2048]{0:T(1024)S(1)} %bitcast.64, f32[2048]{0:T(1024)S(1)} %bitcast.65, ...), kind=kOutput, calls=%fused_computation.58 | convolution fusion | flops 4330618880 | bytes 77725696 | tf_op jit(solution)/shard_map/dot_general | solution.py:59
  119.9 12.8 %copy.28 = bf16[32,16,2,1024]{0,1,2,3:T(8,128)(2,1)} copy(bf16[32,16,2,1024]{3,1,2,0:T(8,128)(2,1)S(1)} %fusion.34) | data formatting | bytes 4194304 | tf_op jit(solution)/shard_map/convert_element_type | solution.py:62
  132.7 10.1 %reshape.30 = bf16[8,2,65536]{2,1,0:T(2,128)(2,1)S(1)} reshape(bf16[1024,2,16,32]{3,2,1,0:T(8,128)(2,1)} %bitcast.55) | data formatting | bytes 4194304
  142.9 31.9 %all_to_all.18 = bf16[8,2,65536]{2,1,0:T(2,128)(2,1)} all-to-all(bf16[8,2,65536]{2,1,0:T(2,128)(2,1)S(1)} %reshape.30), channel_id=1, replica_groups=mesh['tile'=16,'chan'=8] {'chan'}, dimensions={0} | all-to-all | bytes 4194304 | tf_op jit(solution)/shard_map/all_to_all | solution.py:63
  174.8 8.6 %reshape.31 = bf16[1024,2,16,32]{3,2,1,0:T(8,128)(2,1)} reshape(bf16[8,2,65536]{2,1,0:T(2,128)(2,1)} %all_to_all.18) | data formatting | bytes 4194304
  183.4 10.3 %copy.30 = bf16[32,8,16,2,128]{4,2,1,3,0:T(8,128)(2,1)S(1)} copy(bf16[32,8,16,2,128]{0,2,3,4,1:T(8,128)(2,1)} %bitcast.56) | data formatting | bytes 4194304 | tf_op jit(solution)/shard_map/all_to_all | solution.py:63
  193.7 2.9 copy.31
  196.6 0.0 all-gather.2.cloned.1.call-update
  196.6 3.0 copy.35
  199.6 1.9 fusion.39
  201.5 1.5 maximum_bitcast_fusion
  203.1 165.1 %all-gather.2.cloned.1.call-done = bf16[512,128,2,128]{1,0,2,3:T(8,128)(2,1)} async-done(((bf16[32,128,2,128]{1,0,2,3:T(8,128)(2,1)}), bf16[512,128,2,128]{1,0,2,3:T(8,128)(2,1)}) %all-gather.2.cloned.1.call-update) | async-done | bytes 33554448 | tf_op jit(solution)/shard_map/all_gather | solution.py:71
  368.1 0.0 copy-done.2
  368.1 21.9 %fusion.2 = f32[2,128,32,512]{3,2,0,1:T(8,128)} fusion(bf16[512,128,2,128]{1,0,2,3:T(8,128)(2,1)} %all-gather.2.cloned.1.call-done, bf16[1,32,128,2,128]{2,1,3,0,4:T(8,128)(2,1)} %maximum_bitcast_fusion, bf16[1,32,128,2,128]{2,1,3,0,4:T(8,128)(2,1)S(1)} %copy-done.2), kind=kOutput, calls=%fused_computation.3 | convolution fusion | flops 2160066560 | bytes 54525952 | tf_op jit(solution)/shard_map/qaspc,bspc->qcab/dot_general | solution.py:68
  390.1 12.4 %copy.36 = f32[2,128,32,512]{3,2,1,0:T(8,128)} copy(f32[2,128,32,512]{3,2,0,1:T(8,128)} %fusion.2) | data formatting | bytes 33554432 | tf_op jit(solution)/shard_map/mul | solution.py:68
  (2 shorter events, 0.0 us)
Async XLA Ops:
  6.5 9.3 %copy-start.3 = (s32[16,2048]{1,0:T(8,128)S(1)}, s32[16,2048]{1,0:T(8,128)}, u32[]{:S(2)}) copy-start(s32[16,2048]{1,0:T(8,128)} %param.5) | copy-start | bytes 393220
  6.5 361.6 %all-gather.2.cloned.1.call-start = ((), (), s32[]{:S(2)}) async-start(), calls=%async_computation.1 | async-start | bytes 35651584 | tf_op jit(solution)/shard_map/all_gather | solution.py:71
  6.5 9.5 %copy-start.1 = (s32[32,32768]{1,0:T(8,128)S(1)}, s32[32,32768]{1,0:T(8,128)}, u32[]{:S(2)}) copy-start(s32[32,32768]{1,0:T(8,128)} %param.3) | copy-start | bytes 12582916
  10.3 51.4 %collective-permute-start = (bf16[32,30720]{1,0:T(8,128)(2,1)}, bf16[32,30720]{1,0:T(8,128)(2,1)S(1)}, u32[]{:S(2)}, u32[]{:S(2)}) collective-permute-start(bf16[32,30720]{1,0:T(8,128)(2,1)} %slice_convert_fusion), channel_id=1, source_target_pairs={{0,1},{1,2},{2,3},{3,4},{4,5},{5,6},{6,7},{8,9},{9,10},{10,11},{11... | collective-permute-start | bytes 5898248 | tf_op jit(solution)/shard_map/ppermute | solution.py:16
  61.7 3.4 copy-start
  199.6 168.5 %copy-start.2 = (bf16[1,32,128,2,128]{2,1,3,0,4:T(8,128)(2,1)S(1)}, bf16[1,32,128,2,128]{2,1,3,0,4:T(8,128)(2,1)}, u32[]{:S(2)}) copy-start(bf16[1,32,128,2,128]{2,1,3,0,4:T(8,128)(2,1)} %copy.35) | copy-start | bytes 6291460
Sparse Core Ops, SparseCore 0:
  196.8 171.3 all-gather.1
where the time goes:
time: 410 us; the launch traced here: 409 us
  waiting for transfers between devices  165 us (40%)
  local copies, waits for them, and re-layouts  68.6 us (17%)
  matrix products  65.5 us (16%)
  other arithmetic  59.2 us (14%)
  blocking collectives  31.9 us (8%)
  between operations  13.5 us (3%)
  starting transfers between devices  5.58 us (1%)
    all_gather x1, waiting for transfers between devices, body(): lax.all_gather(turned, 'tile', axis=0, tiled=True)  165 us
    dot_general x1, matrix products, body(): jnp.dot(filtered.reshape(-1, FFT), dft_table(FFT, CH), preferred_element_...  43.5 us
    another operation x2, other arithmetic  38.7 us
    all_to_all x1, blocking collectives, body(): lax.all_to_all(spectra, 'chan', split_axis=3, concat_axis=1, tiled=True)  31.9 us
    dot_general x1, matrix products, body(): jnp.einsum('qaspc,bspc->qcab', row_sets, lax.all_gather(turned, 'tile', a...  21.9 us
    unnamed x10, local copies, waits for them, and re-layouts  19.5 us
    all_to_all x2, local copies, waits for them, and re-layouts, body(): lax.all_to_all(spectra, 'chan', split_axis=3, concat_axis=1, tiled=True)  13.2 us
    convert_element_type x1, local copies, waits for them, and re-layouts, body(): spectra.reshape(local_inputs, spectra_count, 2, CH).astype(jnp.bfloat16)  12.8 us
  transfers between devices with their start and end apart: 2, of which 1 were waited for; matrix products, arithmetic and copies ran while one was open for 13% of the time, Pallas kernels for 0%

commit v1 on v0

--- a/solution.py
+++ b/solution.py
@@ -68,7 +68,15 @@
         jnp.einsum(
             "qaspc,bspc->qcab",
             row_sets,
-            lax.all_gather(turned, "tile", axis=0, tiled=True),
+            jnp.concatenate(
+                lax.all_to_all(
+                    jnp.stack([turned for _ in range(lax.axis_size("tile"))], axis=0),
+                    axis_name="tile",
+                    split_axis=0,
+                    concat_axis=0,
+                ),
+                axis=0,
+            ),
             preferred_element_type=jnp.float32,
         )
         * average

time: 410 us -> 793 us (1.93)
  waiting for transfers between devices: 165 us -> 519 us
  local copies, waits for them, and re-layouts: 68.6 us -> 106 us
  between operations: 13.5 us -> 0.09 us
  starting transfers between devices: 5.58 us -> 13.9 us
    all_to_all x0 -> x1, waiting for transfers between devices: none -> 519 us  [body(): lax.all_to_all(jnp.stack([turned for _ in range(lax.axis_size('tile'))],...]
    all_gather x1 -> x0, waiting for transfers between devices: 165 us -> none  [body(): lax.all_gather(turned, 'tile', axis=0, tiled=True)]
    all_to_all x0 -> x1, local copies, waits for them, and re-layouts: none -> 23.1 us  [body(): lax.all_to_all(jnp.stack([turned for _ in range(lax.axis_size('tile'))],...]
    another operation x1 -> x3, local copies, waits for them, and re-layouts: 2.97 us -> 19.5 us  [body(): jnp.stack([turned for _ in range(lax.axis_size('tile'))], axis=0)]
    all_to_all x0 -> x1, starting transfers between devices: none -> 8.34 us  [body(): lax.all_to_all(jnp.stack([turned for _ in range(lax.axis_size('tile'))],...]
  transfers between devices with their start and end apart: 2 -> 2, of which waited for: 1 -> 1; matrix products, arithmetic and copies ran while one was open for 13% -> 7% of each run, Pallas kernels for 0% -> 0%
where the time goes in v1:
time: 793 us; the launch traced here: 792 us
  waiting for transfers between devices  519 us (65%)
  local copies, waits for them, and re-layouts  106 us (13%)
  matrix products  63.3 us (8%)
  other arithmetic  57.5 us (7%)
  blocking collectives  31.9 us (4%)
  starting transfers between devices  13.9 us (2%)
    all_to_all x1, waiting for transfers between devices, body(): lax.all_to_all(jnp.stack([turned for _ in range(lax.axis_size('tile'))],...  519 us
    dot_general x1, matrix products, body(): jnp.dot(filtered.reshape(-1, FFT), dft_table(FFT, CH), preferred_element_...  41.3 us
    another operation x2, other arithmetic  38.7 us
    all_to_all x1, blocking collectives, body(): lax.all_to_all(spectra, 'chan', split_axis=3, concat_axis=1, tiled=True)  31.9 us
    all_to_all x1, local copies, waits for them, and re-layouts, body(): lax.all_to_all(jnp.stack([turned for _ in range(lax.axis_size('tile'))],...  23.1 us
    dot_general x1, matrix products, body(): jnp.einsum('qaspc,bspc->qcab', row_sets, jnp.concatenate(lax.all_to_all(j...  22 us
    another operation x3, local copies, waits for them, and re-layouts, body(): jnp.stack([turned for _ in range(lax.axis_size('tile'))], axis=0)  19.5 us
    unnamed x10, local copies, waits for them, and re-layouts  19.5 us
  transfers between devices with their start and end apart: 2, of which 1 were waited for; matrix products, arithmetic and copies ran while one was open for 7% of the time, Pallas kernels for 0%

profile of v1, /device:TPU:1, one launch (start us, length us, event | category | flops | bytes accessed | tf_op | source)
XLA Modules:
  0.0 791.7 jit_solution(9043852639359704026)
XLA Ops:
  0.0 0.0 copy-start.1
  0.0 0.0 copy-start.3
  0.0 3.8 slice_convert_fusion
  3.8 5.6 collective-permute-start
  9.3 0.0 copy-done.3
  9.4 0.1 fusion.36
  9.5 0.0 copy-done.1
  9.5 2.2 convert_element_type.28
  11.7 34.9 %multiply_convert_fusion = (bf16[2048,1024]{0,1:T(8,128)(2,1)}, bf16[2048,1024]{0,1:T(8,128)(2,1)}) fusion(), kind=kLoop, calls=%fused_computation.9 | loop fusion | flops 39845888 | bytes 8388608 | tf_op jit(solution)/shard_map/convert.1
  46.6 8.5 %pad_maximum_fusion = bf16[2048,2048]{0,1:T(8,128)(2,1)} fusion(bf16[2048,1024]{0,1:T(8,128)(2,1)} %get-tuple-element.23, bf16[2048,1024]{0,1:T(8,128)(2,1)} %get-tuple-element.24), kind=kLoop, calls=%fused_computation.8 | loop fusion | flops 16777216 | bytes 16777216 | tf_op jit(solution)/shard_map/concatenate | solution.py:24
  55.2 0.0 collective-permute-done
  55.2 2.6 convert_select_fusion
  57.8 0.7 copy-done
  58.5 3.7 pad_maximum_fusion.1
  62.2 7.6 reshape.30
  69.8 41.3 %fusion.30 = bf16[32,16,2,1024]{3,1,2,0:T(8,128)(2,1)S(1)} fusion(bf16[2,1024,2048,1]{2,1,0,3:T(8,128)(2,1)} %bitcast.59, f32[32,31,2048]{2,1,0:T(8,128)} %reshape.30, f32[2048]{0:T(1024)S(1)} %bitcast.61, f32[2048]{0:T(1024)S(1)} %bitcast.62, f32[2048]{0:T(1024)S(1)} %bitcast.63, f32[2048]{0:T(1024)S(1)} %bitcast.64, f32[2048]{0:T(1024)S(1)} %bitcast.65, ...), kind=kOutput, calls=%fused_computation.56 | convolution fusion | flops 4330618880 | bytes 77725696 | tf_op jit(solution)/shard_map/dot_general | solution.py:59
  111.2 12.8 %copy.30 = bf16[32,16,2,1024]{0,1,2,3:T(8,128)(2,1)} copy(bf16[32,16,2,1024]{3,1,2,0:T(8,128)(2,1)S(1)} %fusion.30) | data formatting | bytes 4194304 | tf_op jit(solution)/shard_map/convert_element_type | solution.py:62
  124.0 10.1 %reshape.36 = bf16[8,2,65536]{2,1,0:T(2,128)(2,1)S(1)} reshape(bf16[1024,2,16,32]{3,2,1,0:T(8,128)(2,1)} %bitcast.55) | data formatting | bytes 4194304
  134.2 31.9 %all_to_all.20 = bf16[8,2,65536]{2,1,0:T(2,128)(2,1)} all-to-all(bf16[8,2,65536]{2,1,0:T(2,128)(2,1)S(1)} %reshape.36), channel_id=1, replica_groups=mesh['tile'=16,'chan'=8] {'chan'}, dimensions={0} | all-to-all | bytes 4194304 | tf_op jit(solution)/shard_map/all_to_all | solution.py:63
  166.1 8.6 %reshape.37 = bf16[1024,2,16,32]{3,2,1,0:T(8,128)(2,1)} reshape(bf16[8,2,65536]{2,1,0:T(2,128)(2,1)} %all_to_all.20) | data formatting | bytes 4194304
  174.7 11.3 %copy.32 = bf16[32,8,16,2,128]{4,2,1,3,0:T(8,128)(2,1)} copy(bf16[32,8,16,2,128]{0,2,3,4,1:T(8,128)(2,1)} %bitcast.56) | data formatting | bytes 4194304 | tf_op jit(solution)/shard_map/all_to_all | solution.py:63
  186.0 3.5 copy.33
  189.5 11.4 %stack.13 = bf16[16,32,128,2,128]{2,1,3,4,0:T(8,128)(2,1)} broadcast(bf16[32,128,2,128]{1,0,2,3:T(8,128)(2,1)S(1)} %copy.33), dimensions={1,2,3,4} | broadcast | bytes 35651584 | tf_op jit(solution)/shard_map/stack | solution.py:73
  200.9 8.3 %all-to-all-start.1 = ((bf16[16,32,128,2,128]{2,1,3,4,0:T(8,128)(2,1)}), bf16[16,32,128,2,128]{2,1,3,4,0:T(8,128)(2,1)}, u32[]{:S(2)}, u32[]{:S(2)}) async-start(bf16[16,32,128,2,128]{2,1,3,4,0:T(8,128)(2,1)} %stack.13), calls=%async_computation.1 | async-start | bytes 67108864 | tf_op jit(solution)/shard_map/all_to_all | solution.py:72
  209.2 4.6 copy.38
  213.8 0.2 fusion.35
  214.0 1.5 maximum_bitcast_fusion
  215.5 518.6 %all-to-all-done.1 = bf16[16,32,128,2,128]{2,1,3,4,0:T(8,128)(2,1)} async-done(((bf16[16,32,128,2,128]{2,1,3,4,0:T(8,128)(2,1)}), bf16[16,32,128,2,128]{2,1,3,4,0:T(8,128)(2,1)}, u32[]{:S(2)}, u32[]{:S(2)}) %all-to-all-start.1) | async-done | bytes 33554464 | tf_op jit(solution)/shard_map/all_to_all | solution.py:72
  734.2 23.1 %copy.34 = bf16[16,32,128,2,128]{2,1,0,3,4:T(8,128)(2,1)} copy(bf16[16,32,128,2,128]{2,1,3,4,0:T(8,128)(2,1)} %all-to-all-done.1) | data formatting | bytes 67108864 | tf_op jit(solution)/shard_map/all_to_all | solution.py:72
  757.3 0.0 copy-done.2
  757.3 22.0 %fusion = f32[2,128,32,512]{3,2,0,1:T(8,128)} fusion(bf16[512,128,2,128,1]{1,0,2,4,3:T(8,128)(2,1)} %bitcast.54, bf16[1,32,128,2,128]{2,1,3,0,4:T(8,128)(2,1)} %maximum_bitcast_fusion, bf16[1,32,128,2,128]{2,1,3,0,4:T(8,128)(2,1)S(1)} %copy-done.2), kind=kOutput, calls=%fused_computation.1 | convolution fusion | flops 2160066560 | bytes 54525952 | tf_op jit(solution)/shard_map/qaspc,bspc->qcab/dot_general | solution.py:68
  779.3 12.4 %copy.39 = f32[2,128,32,512]{3,2,1,0:T(8,128)} copy(f32[2,128,32,512]{3,2,0,1:T(8,128)} %fusion) | data formatting | bytes 33554432 | tf_op jit(solution)/shard_map/mul | solution.py:68
  (3 shorter events, 0.0 us)
Async XLA Ops:
  0.0 9.5 %copy-start.1 = (s32[32,32768]{1,0:T(8,128)S(1)}, s32[32,32768]{1,0:T(8,128)}, u32[]{:S(2)}) copy-start(s32[32,32768]{1,0:T(8,128)} %param.3) | copy-start | bytes 12582916
  0.0 9.3 %copy-start.3 = (s32[16,2048]{1,0:T(8,128)S(1)}, s32[16,2048]{1,0:T(8,128)}, u32[]{:S(2)}) copy-start(s32[16,2048]{1,0:T(8,128)} %param.5) | copy-start | bytes 393220
  3.8 51.4 %collective-permute-start = (bf16[32,30720]{1,0:T(8,128)(2,1)}, bf16[32,30720]{1,0:T(8,128)(2,1)S(1)}, u32[]{:S(2)}, u32[]{:S(2)}) collective-permute-start(bf16[32,30720]{1,0:T(8,128)(2,1)} %slice_convert_fusion), channel_id=1, source_target_pairs={{0,1},{1,2},{2,3},{3,4},{4,5},{5,6},{6,7},{8,9},{9,10},{10,11},{11... | collective-permute-start | bytes 5898248 | tf_op jit(solution)/shard_map/ppermute | solution.py:16
  55.2 3.4 copy-start
  200.9 533.3 %all-to-all-start.1 = ((bf16[16,32,128,2,128]{2,1,3,4,0:T(8,128)(2,1)}), bf16[16,32,128,2,128]{2,1,3,4,0:T(8,128)(2,1)}, u32[]{:S(2)}, u32[]{:S(2)}) async-start(bf16[16,32,128,2,128]{2,1,3,4,0:T(8,128)(2,1)} %stack.13), calls=%async_computation.1 | async-start | bytes 67108864 | tf_op jit(solution)/shard_map/all_to_all | solution.py:72
  215.5 541.7 %copy-start.2 = (bf16[1,32,128,2,128]{2,1,3,0,4:T(8,128)(2,1)S(1)}, bf16[1,32,128,2,128]{2,1,3,0,4:T(8,128)(2,1)}, u32[]{:S(2)}) copy-start(bf16[1,32,128,2,128]{2,1,3,0,4:T(8,128)(2,1)} %copy.38) | copy-start | bytes 6291460
